TPU v7x, 512 devices: a whole 4x8x8 slice. The times are simulated.
512 devices in a mesh: blk: 16 (over z, y_lo), tan: 32 (over y_hi, x, core).
Axes of the slice: x: 4, y: 8 (y_hi: 4, y_lo: 2; y = y_hi * 2 + y_lo), z: 8, core: 2. Of those that a mesh axis runs over, the one named last changes fastest.
Arguments:
- layer_in: bfloat16 [2048, 256], P('blk'), may hold values from -6 to 6
- laplace_in: bfloat16 [2048, 256], P('blk'), may hold values from -6 to 6
- tangent_in: bfloat16 [2048, 64, 256], P('blk', 'tan'), may hold values from -1.5 to 1.5
- spin_labels: int32 [2048], P('blk'), may hold values from 0 to 1
- pair_bias: bfloat16 [2048, 2048], P('blk'), may hold values from -6 to 306
- query_weight: bfloat16 [256, 256], replicated, may hold values from -0.375 to 0.375
- key_weight: bfloat16 [256, 256], replicated, may hold values from -0.375 to 0.375
- value_weight: bfloat16 [256, 256], replicated, may hold values from -0.375 to 0.375
- out_weight: bfloat16 [256, 256], replicated, may hold values from -0.375 to 0.375
- head_gain: float32 [4], replicated, may hold values from 0.5 to 2
- spin_gain: float32 [4], replicated, may hold values from -2 to 2
Outputs:
- layer_out: bfloat16 [2048, 256], P('blk')
- tangent_out: bfloat16 [2048, 64, 256], P('blk', 'tan')
- laplacian_out: float32 [2048, 256], P('blk')
All inputs are finite; a program needn't handle non-finite values.
Results may differ from a plain program's by a relative error of at most 0.02.
Values may be sent and summed in bfloat16 or wider, within the bound.
A program may use at most 64 MiB of HBM per device.

v0:
```python
import math
import jax
import jax.numpy as jnp
from jax import lax
from jax.sharding import PartitionSpec as P


def project(rows, weight):
    return jnp.dot(rows, weight, preferred_element_type=jnp.float32).astype(jnp.bfloat16)


def project_tangent(tangent, weight):
    count, dirs, width = tangent.shape
    return project(tangent.reshape(count * dirs, width), weight).reshape(count, dirs, width)


def on_device(
    layer_in,
    laplace_in,
    tangent_in,
    spin_labels,
    pair_bias,
    query_weight,
    key_weight,
    value_weight,
    out_weight,
    head_gain,
    spin_gain,
):
    rows, width = layer_in.shape
    heads = head_gain.shape[0]
    head_size = width // heads
    dirs = tangent_in.shape[1]
    scale = 1.0 / math.sqrt(head_size)
    bias_cols = lax.all_to_all(pair_bias, "blk", split_axis=1, concat_axis=0, tiled=True)
    query = project(layer_in, query_weight).reshape(rows, heads, head_size)
    lap_query = project(laplace_in, query_weight).reshape(rows, heads, head_size)
    tan_query = project_tangent(tangent_in, query_weight).reshape(rows, dirs, heads, head_size)
    spin_query = spin_labels.astype(jnp.float32)
    spin_wire = spin_labels.astype(jnp.bfloat16)

    def attend(carry, block, first):
        top, total, numer, tan_total, tan_numer, lap_total, lap_numer, trace_total, trace_numer = (
            carry
        )
        key_b, value_b, lap_key_b, lap_value_b, tan_key_b, tan_value_b, spin_key = block
        count = key_b.shape[0]
        key_h = key_b.reshape(count, heads, head_size)
        value_h = value_b.reshape(count, heads, head_size)
        lap_key_h = lap_key_b.reshape(count, heads, head_size)
        lap_value_h = lap_value_b.reshape(count, heads, head_size)
        tan_key_h = tan_key_b.reshape(count, dirs, heads, head_size)
        tan_value_h = tan_value_b.reshape(count, dirs, heads, head_size)
        bias_rows = lax.dynamic_slice_in_dim(bias_cols, first, count, 0).astype(jnp.float32)
        spin_float = spin_key.astype(jnp.float32)
        same = (
            spin_query[:, None] * spin_float[None, :]
            + (1.0 - spin_query)[:, None] * (1.0 - spin_float)[None, :]
        )
        scores = (
            jnp.einsum("ihd,jhd->hij", query, key_h, preferred_element_type=jnp.float32) * scale
        )
        scores = (
            scores
            + head_gain[:, None, None] * bias_rows.T[None]
            + spin_gain[:, None, None] * same[None]
        )
        new_top = jnp.maximum(top, jnp.max(scores, axis=2))
        shrink = jnp.exp(top - new_top)
        shrink_rows = shrink.T[:, :, None]
        unnorm = jnp.exp(scores - new_top[:, :, None])
        weights = unnorm.astype(jnp.bfloat16)
        total = total * shrink + jnp.sum(unnorm, axis=2)
        numer = numer * shrink_rows + jnp.einsum(
            "hij,jhd->ihd", weights, value_h, preferred_element_type=jnp.float32
        )
        lap_scores = (
            jnp.einsum("ihd,jhd->hij", lap_query, key_h, preferred_element_type=jnp.float32)
            + jnp.einsum("ihd,jhd->hij", query, lap_key_h, preferred_element_type=jnp.float32)
        ) * scale
        lap_weighted = unnorm * lap_scores
        lap_total = lap_total * shrink + jnp.sum(lap_weighted, axis=2)
        lap_numer = (
            lap_numer * shrink_rows
            + jnp.einsum(
                "hij,jhd->ihd",
                lap_weighted.astype(jnp.bfloat16),
                value_h,
                preferred_element_type=jnp.float32,
            )
            + jnp.einsum("hij,jhd->ihd", weights, lap_value_h, preferred_element_type=jnp.float32)
        )
        tan_scores = (
            jnp.einsum("iahd,jhd->ahij", tan_query, key_h, preferred_element_type=jnp.float32)
            + jnp.einsum("ihd,jahd->ahij", query, tan_key_h, preferred_element_type=jnp.float32)
        ) * scale
        cross = (
            jnp.einsum("iahd,jahd->ahij", tan_query, tan_key_h, preferred_element_type=jnp.float32)
            * scale
        )
        tan_weighted = unnorm[None] * tan_scores
        tan_weights = tan_weighted.astype(jnp.bfloat16)
        tan_total = tan_total * shrink[None] + jnp.sum(tan_weighted, axis=3)
        tan_numer = (
            tan_numer * shrink_rows[:, None]
            + jnp.einsum("ahij,jhd->iahd", tan_weights, value_h, preferred_element_type=jnp.float32)
            + jnp.einsum("hij,jahd->iahd", weights, tan_value_h, preferred_element_type=jnp.float32)
        )
        second = unnorm[None] * (tan_scores * tan_scores + 2.0 * cross)
        trace_total = trace_total * shrink + jnp.sum(second, axis=(0, 3))
        trace_numer = (
            trace_numer * shrink_rows
            + jnp.einsum(
                "ahij,jhd->ihd",
                second.astype(jnp.bfloat16),
                value_h,
                preferred_element_type=jnp.float32,
            )
            + 2.0
            * jnp.einsum(
                "ahij,jahd->ihd", tan_weights, tan_value_h, preferred_element_type=jnp.float32
            )
        )
        return (
            new_top,
            total,
            numer,
            tan_total,
            tan_numer,
            lap_total,
            lap_numer,
            trace_total,
            trace_numer,
        )

    head_zeros = jnp.zeros((heads, rows), jnp.float32)
    row_zeros = jnp.zeros((rows, heads, head_size), jnp.float32)
    start_carry = (
        jnp.full((heads, rows), -1e30, jnp.float32),
        head_zeros,
        row_zeros,
        jnp.zeros((dirs, heads, rows), jnp.float32),
        jnp.zeros((rows, dirs, heads, head_size), jnp.float32),
        head_zeros,
        row_zeros,
        head_zeros,
        row_zeros,
    )
    own_keys = project(layer_in, key_weight)
    own_values = project(layer_in, value_weight)
    own_lap_keys = project(laplace_in, key_weight)
    own_lap_values = project(laplace_in, value_weight)
    own_tan_keys = project_tangent(tangent_in, key_weight)
    own_tan_values = project_tangent(tangent_in, value_weight)
    block = (
        lax.all_gather(own_keys, "blk", axis=0, tiled=True),
        lax.all_gather(own_values, "blk", axis=0, tiled=True),
        lax.all_gather(own_lap_keys, "blk", axis=0, tiled=True),
        lax.all_gather(own_lap_values, "blk", axis=0, tiled=True),
        lax.all_gather(own_tan_keys, "blk", axis=0, tiled=True),
        lax.all_gather(own_tan_values, "blk", axis=0, tiled=True),
        lax.all_gather(spin_wire, "blk", axis=0, tiled=True),
    )
    count = block[0].shape[0]
    size = 256
    parts = count // size
    stacked = tuple((piece.reshape((parts, size) + piece.shape[1:]) for piece in block))

    def step(inner, item):
        number, pieces = item
        return (attend(inner, pieces, number * size), None)

    result, _ = lax.scan(step, start_carry, (jnp.arange(parts, dtype=jnp.int32), stacked))
    top, total, numer, tan_total, tan_numer, lap_total, lap_numer, trace_total, trace_numer = result
    denom = total.T[:, :, None]
    denom_sq = denom * denom
    attn = numer / denom
    tan_denom = jnp.transpose(tan_total, (2, 0, 1))[..., None]
    attn_tan = tan_numer / denom[:, None] - numer[:, None] * tan_denom / denom_sq[:, None]
    cross_sum = jnp.sum(tan_numer * tan_denom, axis=1)
    square_sum = jnp.sum(tan_denom * tan_denom, axis=1)
    own_terms = (
        trace_numer / denom
        - numer * trace_total.T[:, :, None] / denom_sq
        - 2.0 * cross_sum / denom_sq
        + 2.0 * numer * square_sum / (denom_sq * denom)
    )
    shared = lax.psum(own_terms.reshape(rows, width).astype(jnp.bfloat16), "tan").astype(
        jnp.float32
    )
    attn_lap = (lap_numer / denom - numer * lap_total.T[:, :, None] / denom_sq).reshape(
        rows, width
    ) + shared
    layer_out = (
        jnp.dot(
            attn.reshape(rows, width).astype(jnp.bfloat16),
            out_weight,
            preferred_element_type=jnp.float32,
        )
        + layer_in.astype(jnp.float32)
    ).astype(jnp.bfloat16)
    tan_flat = attn_tan.reshape(rows * dirs, width).astype(jnp.bfloat16)
    tangent_out = jnp.dot(tan_flat, out_weight, preferred_element_type=jnp.float32).reshape(
        rows, dirs, width
    )
    tangent_out = (tangent_out + tangent_in.astype(jnp.float32)).astype(jnp.bfloat16)
    laplacian_out = jnp.dot(
        attn_lap.astype(jnp.bfloat16), out_weight, preferred_element_type=jnp.float32
    ) + laplace_in.astype(jnp.float32)
    return (layer_out, tangent_out, laplacian_out)


def solution(mesh):
    in_specs = (
        P("blk", None),
        P("blk", None),
        P("blk", "tan", None),
        P("blk"),
        P("blk", None),
        P(),
        P(),
        P(),
        P(),
        P(),
        P(),
    )
    out_specs = (P("blk", None), P("blk", "tan", None), P("blk", None))
    return jax.shard_map(
        on_device, mesh=mesh, in_specs=in_specs, out_specs=out_specs, check_vma=False
    )
```

profile of v0, /device:TPU:8, one launch (start us, length us, event | category | flops | bytes accessed | tf_op | source)
XLA Modules:
  0.0 942.7 jit_solution(8929567075966488008)
XLA Ops:
  7.2 1.8 convolution_convert_fusion.8
  9.1 1.7 convolution_convert_fusion.3
  10.9 1.7 convolution_convert_fusion.6
  12.7 1.7 convolution_convert_fusion.4
  19.4 11.8 %all-to-all-start = ((bf16[128,16,128]{2,0,1:T(8,128)(2,1)}), bf16[128,16,128]{2,0,1:T(8,128)(2,1)}, u32[]{:S(2)}, u32[]{:S(2)}) async-start(bf16[128,16,128]{2,0,1:T(8,128)(2,1)} %copy_bitcast_fusion), calls=%async_computation | async-start | bytes 1048576 | tf_op jit(solution)/shard_map/all_to_all | solution.py:35
  32.5 34.9 %all-gather = bf16[16,1,128]{2,1,0:T(2,128)(2,1)S(1)} all-gather(bf16[1,1,128]{2,1,0:T(2,128)(2,1)S(1)} %get-tuple-element.593), channel_id=1, replica_groups=mesh['blk'=16,'tan'=32] {'blk'}, dimensions={0}, use_global_device_ids=true | all-gather | bytes 4352 | tf_op jit(solution)/shard_map/all_gather | solution.py:162
  69.9 20.5 %all-gather.8.cloned.1.call-done = bf16[2048,256]{1,0:T(8,128)(2,1)} async-done(((bf16[128,256]{1,0:T(8,128)(2,1)}), bf16[2048,256]{1,0:T(8,128)(2,1)}) %all-gather.8.cloned.1.call-update) | async-done | bytes 1048592 | tf_op jit(solution)/shard_map/all_gather | solution.py:156
  90.4 74.6 %all-gather.18.cloned.1.call-done = bf16[2048,256]{1,0:T(8,128)(2,1)} async-done(((bf16[128,256]{1,0:T(8,128)(2,1)}), bf16[2048,256]{1,0:T(8,128)(2,1)}) %all-gather.18.cloned.1.call-update) | async-done | bytes 1048592 | tf_op jit(solution)/shard_map/all_gather | solution.py:159
  165.0 75.4 %all-gather.10.cloned.1.call-done = bf16[2048,256]{1,0:T(8,128)(2,1)} async-done(((bf16[128,256]{1,0:T(8,128)(2,1)}), bf16[2048,256]{1,0:T(8,128)(2,1)}) %all-gather.10.cloned.1.call-update) | async-done | bytes 1048592 | tf_op jit(solution)/shard_map/all_gather | solution.py:157
  240.4 75.2 %all-gather.16.cloned.1.call-done = bf16[2048,256]{1,0:T(8,128)(2,1)} async-done(((bf16[128,256]{1,0:T(8,128)(2,1)}), bf16[2048,256]{1,0:T(8,128)(2,1)}) %all-gather.16.cloned.1.call-update) | async-done | bytes 1048592 | tf_op jit(solution)/shard_map/all_gather | solution.py:158
  315.6 80.3 %all-gather.12.cloned.1.call-done = bf16[2048,2,256]{2,0,1:T(8,128)(2,1)} async-done(((bf16[128,2,256]{2,0,1:T(8,128)(2,1)}), bf16[2048,2,256]{2,0,1:T(8,128)(2,1)}) %all-gather.12.cloned.1.call-update) | async-done | bytes 2097168 | tf_op jit(solution)/shard_map/all_gather | solution.py:160
  395.9 79.9 %all-gather.14.cloned.1.call-done = bf16[2048,2,256]{2,0,1:T(8,128)(2,1)} async-done(((bf16[128,2,256]{2,0,1:T(8,128)(2,1)}), bf16[2048,2,256]{2,0,1:T(8,128)(2,1)}) %all-gather.14.cloned.1.call-update) | async-done | bytes 2097168 | tf_op jit(solution)/shard_map/all_gather | solution.py:161
  476.3 194.2 %while.29 = (s32[]{:T(128)}, f32[4,128]{1,0:T(4,128)S(1)}, f32[4,128]{1,0:T(4,128)}, f32[128,4,64]{0,2,1:T(8,128)}, f32[2,4,128]{2,0,1:T(2,128)S(1)}, /*index=5*...) while((s32[]{:T(128)}, f32[4,128]{1,0:T(4,128)S(1)}, ...), condition=%wide.region_7.8_spmd.clone, body=%wide.region_0.7_spmd.clone.sunk | while | flops 325065856 | bytes 26266780 | solution.py:173
  479.9 1.6 constant_dynamic-slice_fusion.10
  486.1 1.5 multiply_convert_fusion.2
  488.6 1.4 convert_reduce_fusion.2
  491.5 1.7 fusion.155
  499.9 1.2 dynamic_slice.87
  503.5 1.6 constant_dynamic-slice_fusion.10
  509.7 1.5 multiply_convert_fusion.2
  512.3 1.4 convert_reduce_fusion.2
  515.8 1.8 fusion.155
  527.9 1.6 constant_dynamic-slice_fusion.10
  534.1 1.5 multiply_convert_fusion.2
  536.6 1.4 convert_reduce_fusion.2
  540.2 1.8 fusion.155
  552.2 1.6 constant_dynamic-slice_fusion.10
  558.5 1.5 multiply_convert_fusion.2
  561.0 1.4 convert_reduce_fusion.2
  564.6 1.8 fusion.155
  576.6 1.6 constant_dynamic-slice_fusion.10
  582.8 1.5 multiply_convert_fusion.2
  585.4 1.4 convert_reduce_fusion.2
  589.0 1.8 fusion.155
  601.0 1.6 constant_dynamic-slice_fusion.10
  607.2 1.5 multiply_convert_fusion.2
  609.7 1.4 convert_reduce_fusion.2
  613.3 1.8 fusion.155
  625.4 1.6 constant_dynamic-slice_fusion.10
  631.6 1.5 multiply_convert_fusion.2
  634.1 1.4 convert_reduce_fusion.2
  637.7 1.8 fusion.155
  649.7 1.6 constant_dynamic-slice_fusion.10
  655.9 1.5 multiply_convert_fusion.2
  658.5 1.4 convert_reduce_fusion.2
  662.1 1.8 fusion.155
  672.4 1.8 add_convert_fusion
  677.1 257.1 %all-reduce.2.cloned.1.call-done = bf16[128,256]{0,1:T(8,128)(2,1)} async-done(((bf16[128,256]{0,1:T(8,128)(2,1)}), bf16[128,256]{0,1:T(8,128)(2,1)}) %all-reduce.2.cloned.1.call-update) | async-done | bytes 65552 | tf_op jit(solution)/shard_map/psum | solution.py:188
  (469 shorter events, 151.2 us)
Async XLA Ops:
  7.2 11.3 %copy-start = (bf16[128,2048]{1,0:T(8,128)(2,1)S(1)}, bf16[128,2048]{1,0:T(8,128)(2,1)}, u32[]{:S(2)}) copy-start(bf16[128,2048]{1,0:T(8,128)(2,1)} %param.17) | copy-start | bytes 1572868
  7.2 10.3 %copy-start.5 = (bf16[256,256]{1,0:T(8,128)(2,1)S(1)}, bf16[256,256]{1,0:T(8,128)(2,1)}, u32[]{:S(2)}) copy-start(bf16[256,256]{1,0:T(8,128)(2,1)} %param.20) | copy-start | bytes 393220
  7.2 83.2 %all-gather.8.cloned.1.call-start = ((), (), s32[]{:S(2)}) async-start(), calls=%async_computation.1 | async-start | bytes 1114112 | tf_op jit(solution)/shard_map/all_gather | solution.py:156
  9.1 155.9 %all-gather.18.cloned.1.call-start = ((), (), s32[]{:S(2)}) async-start(), calls=%async_computation.6 | async-start | bytes 1114112 | tf_op jit(solution)/shard_map/all_gather | solution.py:159
  10.9 229.5 %all-gather.10.cloned.1.call-start = ((), (), s32[]{:S(2)}) async-start(), calls=%async_computation.2 | async-start | bytes 1114112 | tf_op jit(solution)/shard_map/all_gather | solution.py:157
  12.7 302.9 %all-gather.16.cloned.1.call-start = ((), (), s32[]{:S(2)}) async-start(), calls=%async_computation.5 | async-start | bytes 1114112 | tf_op jit(solution)/shard_map/all_gather | solution.py:158
  14.5 381.4 %all-gather.12.cloned.1.call-start = ((), (), s32[]{:S(2)}) async-start(), calls=%async_computation.3 | async-start | bytes 2228224 | tf_op jit(solution)/shard_map/all_gather | solution.py:160
  15.5 15.8 %copy-start.6 = (bf16[256,256]{1,0:T(8,128)(2,1)S(1)}, bf16[256,256]{1,0:T(8,128)(2,1)}, u32[]{:S(2)}) copy-start(bf16[256,256]{1,0:T(8,128)(2,1)} %param.18) | copy-start | bytes 393220
  17.4 15.1 %copy-start.18 = (s32[128]{0:T(128)S(1)}, s32[128]{0:T(128)}, u32[]{:S(2)}) copy-start(s32[128]{0:T(128)} %param.16) | copy-start | bytes 1540
  17.4 50.7 %copy-start.8 = (bf16[128,256]{1,0:T(8,128)(2,1)S(1)}, bf16[128,256]{1,0:T(8,128)(2,1)}, u32[]{:S(2)}) copy-start(bf16[128,256]{1,0:T(8,128)(2,1)} %param.13) | copy-start | bytes 196612
  17.4 458.3 %all-gather.14.cloned.1.call-start = ((), (), s32[]{:S(2)}) async-start(), calls=%async_computation.4 | async-start | bytes 2228224 | tf_op jit(solution)/shard_map/all_gather | solution.py:161
  17.8 51.2 %copy-start.10 = (bf16[128,256]{1,0:T(8,128)(2,1)S(1)}, bf16[128,256]{1,0:T(8,128)(2,1)}, u32[]{:S(2)}) copy-start(bf16[128,256]{1,0:T(8,128)(2,1)} %param.14) | copy-start | bytes 196612
  19.4 50.5 %all-to-all-start = ((bf16[128,16,128]{2,0,1:T(8,128)(2,1)}), bf16[128,16,128]{2,0,1:T(8,128)(2,1)}, u32[]{:S(2)}, u32[]{:S(2)}) async-start(bf16[128,16,128]{2,0,1:T(8,128)(2,1)} %copy_bitcast_fusion), calls=%async_computation | async-start | bytes 1048576 | tf_op jit(solution)/shard_map/all_to_all | solution.py:35
  31.2 902.9 %all-reduce.2.cloned.1.call-start = ((), (), s32[]{:S(2)}) async-start(), calls=%async_computation.7 | async-start | bytes 131072 | tf_op jit(solution)/shard_map/psum | solution.py:188
  476.3 5.2 copy-start.16
  490.0 6.7 copy-start.4
  494.4 3.5 copy-start.1
  499.9 5.2 copy-start.16
  513.6 7.5 copy-start.4
  518.8 3.5 copy-start.1
  521.1 2.3 copy-start.2
  524.3 5.2 copy-start.16
  538.0 7.5 copy-start.4
  543.1 3.5 copy-start.1
  545.5 2.3 copy-start.2
  548.7 5.2 copy-start.16
  562.4 7.5 copy-start.4
  567.5 3.5 copy-start.1
  569.8 2.3 copy-start.2
  573.1 5.2 copy-start.16
  586.7 7.5 copy-start.4
  591.9 3.5 copy-start.1
  594.2 2.3 copy-start.2
  597.4 5.2 copy-start.16
  611.1 7.5 copy-start.4
  616.2 3.5 copy-start.1
  618.6 2.3 copy-start.2
  621.8 5.2 copy-start.16
  635.5 7.5 copy-start.4
  640.6 3.5 copy-start.1
  642.9 2.3 copy-start.2
  646.2 5.2 copy-start.16
  659.8 7.5 copy-start.4
  665.0 3.5 copy-start.1
  667.3 2.3 copy-start.2
  670.5 4.9 copy-start.7
  670.5 4.9 copy-start.9
  670.5 264.5 %copy-start.11 = (bf16[128,256]{1,0:T(8,128)(2,1)S(1)}, bf16[128,256]{1,0:T(8,128)(2,1)}, u32[]{:S(2)}) copy-start(bf16[128,256]{1,0:T(8,128)(2,1)} %param.14) | copy-start | bytes 196612
  (49 other events, 56.8 us)
Sparse Core Ops, SparseCore 0:
  10.7 79.6 all-gather.7
  92.5 72.4 all-gather.17
  167.1 73.2 all-gather.9
  242.3 73.2 all-gather.15
  317.5 78.3 all-gather.11
  397.8 77.8 all-gather.13
  674.3 259.7 all-reduce.1
where the time goes:
time: 947 us; the launch traced here: 943 us
  waiting for transfers between devices  663 us (70%)
  matrix products  112 us (12%)
  local copies, waits for them, and re-layouts  65 us (7%)
  blocking collectives  34.9 us (4%)
  other arithmetic  34.7 us (4%)
  between operations  14.4 us (2%)
  starting transfers between devices  12.1 us (1%)
    psum x1, waiting for transfers between devices, on_device(): lax.psum(own_terms.reshape(rows, width).astype(jnp.bfloat16), 'tan')  257 us
    all_gather x1, waiting for transfers between devices, on_device(): lax.all_gather(own_tan_keys, 'blk', axis=0, tiled=True)  80.3 us
    all_gather x1, waiting for transfers between devices, on_device(): lax.all_gather(own_tan_values, 'blk', axis=0, tiled=True)  79.9 us
    all_gather x1, waiting for transfers between devices, on_device(): lax.all_gather(own_values, 'blk', axis=0, tiled=True)  75.4 us
    all_gather x1, waiting for transfers between devices, on_device(): lax.all_gather(own_lap_keys, 'blk', axis=0, tiled=True)  75.2 us
    all_gather x1, waiting for transfers between devices, on_device(): lax.all_gather(own_lap_values, 'blk', axis=0, tiled=True)  74.6 us
    dynamic_slice x80, local copies, waits for them, and re-layouts, on_device(): lax.scan(step, start_carry, (jnp.arange(parts, dtype=jnp.int32), stacked))  52.4 us
    all_gather x1, blocking collectives, on_device(): lax.all_gather(spin_wire, 'blk', axis=0, tiled=True)  34.9 us
  transfers between devices with their start and end apart: 8, of which 7 were waited for; matrix products, arithmetic and copies ran while one was open for 2% of the time, Pallas kernels for 0%

commit v1 on v0

--- a/solution.py
+++ b/solution.py
@@ -3,6 +3,12 @@
 import jax.numpy as jnp
 from jax import lax
 from jax.sharding import PartitionSpec as P
+
+
+def add_all(block, name):
+    pieces = lax.all_gather(block, name, axis=0, tiled=False)
+    result = pieces.sum(axis=0)
+    return result
 
 
 def project(rows, weight):
@@ -185,9 +191,7 @@
         - 2.0 * cross_sum / denom_sq
         + 2.0 * numer * square_sum / (denom_sq * denom)
     )
-    shared = lax.psum(own_terms.reshape(rows, width).astype(jnp.bfloat16), "tan").astype(
-        jnp.float32
-    )
+    shared = add_all(own_terms.reshape(rows, width).astype(jnp.bfloat16), "tan").astype(jnp.float32)
     attn_lap = (lap_numer / denom - numer * lap_total.T[:, :, None] / denom_sq).reshape(
         rows, width
     ) + shared

time: 947 us -> 749 us (0.79)
  the two profiles are of different devices: /device:TPU:8 before, /device:TPU:1 now
where the time goes in v1:
time: 749 us; the launch traced here: 745 us
  waiting for transfers between devices  467 us (62%)
  matrix products  112 us (15%)
  local copies, waits for them, and re-layouts  65.8 us (9%)
  other arithmetic  35.1 us (5%)
  blocking collectives  31.1 us (4%)
  between operations  14.4 us (2%)
  starting transfers between devices  12.3 us (2%)
    all_gather x1, waiting for transfers between devices, on_device(): lax.all_gather(own_tan_keys, 'blk', axis=0, tiled=True)  81.3 us
    all_gather x1, waiting for transfers between devices, on_device(): lax.all_gather(own_tan_values, 'blk', axis=0, tiled=True)  79.9 us
    all_gather x1, waiting for transfers between devices, on_device(): lax.all_gather(own_values, 'blk', axis=0, tiled=True)  75.4 us
    all_gather x1, waiting for transfers between devices, on_device(): lax.all_gather(own_lap_keys, 'blk', axis=0, tiled=True)  75.2 us
    all_gather x1, waiting for transfers between devices, on_device(): lax.all_gather(own_lap_values, 'blk', axis=0, tiled=True)  74.7 us
    all_gather x1, waiting for transfers between devices, add_all(): pieces = lax.all_gather(block, name, axis=0, tiled=False)  65.7 us
    dynamic_slice x80, local copies, waits for them, and re-layouts, on_device(): lax.scan(step, start_carry, (jnp.arange(parts, dtype=jnp.int32), stacked))  52.4 us
    all_gather x1, blocking collectives, on_device(): lax.all_gather(spin_wire, 'blk', axis=0, tiled=True)  31.1 us
  transfers between devices with their start and end apart: 8, of which 7 were waited for; matrix products, arithmetic and copies ran while one was open for 2% of the time, Pallas kernels for 0%

profile of v1, /device:TPU:1, one launch (start us, length us, event | category | flops | bytes accessed | tf_op | source)
XLA Modules:
  0.0 744.7 jit_solution(13933188146281048087)
XLA Ops:
  7.2 1.8 convolution_convert_fusion.8
  9.1 1.7 convolution_convert_fusion.3
  10.9 1.7 convolution_convert_fusion.6
  12.7 1.7 convolution_convert_fusion.4
  19.4 12.0 %all-to-all-start = ((bf16[128,16,128]{2,0,1:T(8,128)(2,1)}), bf16[128,16,128]{2,0,1:T(8,128)(2,1)}, u32[]{:S(2)}, u32[]{:S(2)}) async-start(bf16[128,16,128]{2,0,1:T(8,128)(2,1)} %copy_bitcast_fusion), calls=%async_computation | async-start | bytes 1048576 | tf_op jit(solution)/shard_map/all_to_all | solution.py:41
  32.8 31.1 %all-gather = bf16[16,1,128]{2,1,0:T(2,128)(2,1)S(1)} all-gather(bf16[1,1,128]{2,1,0:T(2,128)(2,1)S(1)} %get-tuple-element.677), channel_id=1, replica_groups=mesh['blk'=16,'tan'=32] {'blk'}, dimensions={0}, use_global_device_ids=true | all-gather | bytes 4352 | tf_op jit(solution)/shard_map/all_gather | solution.py:168
  66.3 15.1 %all-gather.9.cloned.1.call-done = bf16[2048,256]{1,0:T(8,128)(2,1)} async-done(((bf16[128,256]{1,0:T(8,128)(2,1)}), bf16[2048,256]{1,0:T(8,128)(2,1)}) %all-gather.9.cloned.1.call-update) | async-done | bytes 1048592 | tf_op jit(solution)/shard_map/all_gather | solution.py:162
  81.4 74.7 %all-gather.19.cloned.1.call-done = bf16[2048,256]{1,0:T(8,128)(2,1)} async-done(((bf16[128,256]{1,0:T(8,128)(2,1)}), bf16[2048,256]{1,0:T(8,128)(2,1)}) %all-gather.19.cloned.1.call-update) | async-done | bytes 1048592 | tf_op jit(solution)/shard_map/all_gather | solution.py:165
  156.1 75.4 %all-gather.11.cloned.1.call-done = bf16[2048,256]{1,0:T(8,128)(2,1)} async-done(((bf16[128,256]{1,0:T(8,128)(2,1)}), bf16[2048,256]{1,0:T(8,128)(2,1)}) %all-gather.11.cloned.1.call-update) | async-done | bytes 1048592 | tf_op jit(solution)/shard_map/all_gather | solution.py:163
  231.5 75.2 %all-gather.17.cloned.1.call-done = bf16[2048,256]{1,0:T(8,128)(2,1)} async-done(((bf16[128,256]{1,0:T(8,128)(2,1)}), bf16[2048,256]{1,0:T(8,128)(2,1)}) %all-gather.17.cloned.1.call-update) | async-done | bytes 1048592 | tf_op jit(solution)/shard_map/all_gather | solution.py:164
  306.7 81.3 %all-gather.13.cloned.1.call-done = bf16[2048,2,256]{2,0,1:T(8,128)(2,1)} async-done(((bf16[128,2,256]{2,0,1:T(8,128)(2,1)}), bf16[2048,2,256]{2,0,1:T(8,128)(2,1)}) %all-gather.13.cloned.1.call-update) | async-done | bytes 2097168 | tf_op jit(solution)/shard_map/all_gather | solution.py:166
  388.0 79.9 %all-gather.15.cloned.1.call-done = bf16[2048,2,256]{2,0,1:T(8,128)(2,1)} async-done(((bf16[128,2,256]{2,0,1:T(8,128)(2,1)}), bf16[2048,2,256]{2,0,1:T(8,128)(2,1)}) %all-gather.15.cloned.1.call-update) | async-done | bytes 2097168 | tf_op jit(solution)/shard_map/all_gather | solution.py:167
  468.4 194.3 %while.29 = (s32[]{:T(128)}, f32[4,128]{1,0:T(4,128)S(1)}, f32[4,128]{1,0:T(4,128)}, f32[128,4,64]{0,2,1:T(8,128)}, f32[2,4,128]{2,0,1:T(2,128)S(1)}, /*index=5*...) while((s32[]{:T(128)}, f32[4,128]{1,0:T(4,128)S(1)}, ...), condition=%wide.region_7.8_spmd.clone, body=%wide.region_0.7_spmd.clone.sunk | while | flops 325065856 | bytes 26266780 | solution.py:179
  471.9 1.6 constant_dynamic-slice_fusion.10
  478.2 1.5 multiply_convert_fusion.2
  480.7 1.4 convert_reduce_fusion.2
  483.6 1.7 fusion.153
  495.6 1.6 constant_dynamic-slice_fusion.10
  501.8 1.5 multiply_convert_fusion.2
  504.3 1.4 convert_reduce_fusion.2
  507.9 1.8 fusion.153
  516.4 1.2 dynamic_slice.87
  520.0 1.6 constant_dynamic-slice_fusion.10
  526.2 1.5 multiply_convert_fusion.2
  528.7 1.4 convert_reduce_fusion.2
  532.3 1.8 fusion.153
  544.3 1.6 constant_dynamic-slice_fusion.10
  550.5 1.5 multiply_convert_fusion.2
  553.1 1.4 convert_reduce_fusion.2
  556.7 1.8 fusion.153
  568.7 1.6 constant_dynamic-slice_fusion.10
  574.9 1.5 multiply_convert_fusion.2
  577.5 1.4 convert_reduce_fusion.2
  581.0 1.8 fusion.153
  593.1 1.6 constant_dynamic-slice_fusion.10
  599.3 1.5 multiply_convert_fusion.2
  601.8 1.4 convert_reduce_fusion.2
  605.4 1.8 fusion.153
  617.5 1.6 constant_dynamic-slice_fusion.10
  623.7 1.5 multiply_convert_fusion.2
  626.2 1.4 convert_reduce_fusion.2
  629.8 1.8 fusion.153
  641.8 1.6 constant_dynamic-slice_fusion.10
  648.0 1.5 multiply_convert_fusion.2
  650.6 1.4 convert_reduce_fusion.2
  654.2 1.8 fusion.153
  669.4 65.7 %all-gather.21.cloned.1.call-done = bf16[32,128,256]{2,1,0:T(8,128)(2,1)} async-done(((bf16[1,128,256]{2,1,0:T(8,128)(2,1)}), bf16[32,128,256]{2,1,0:T(8,128)(2,1)}) %all-gather.21.cloned.1.call-update) | async-done | bytes 2097168 | tf_op jit(solution)/shard_map/all_gather | solution.py:9
  735.1 1.9 reduce_sum.92
  (471 shorter events, 152.3 us)
Async XLA Ops:
  7.2 11.3 %copy-start = (bf16[128,2048]{1,0:T(8,128)(2,1)S(1)}, bf16[128,2048]{1,0:T(8,128)(2,1)}, u32[]{:S(2)}) copy-start(bf16[128,2048]{1,0:T(8,128)(2,1)} %param.17) | copy-start | bytes 1572868
  7.2 10.3 %copy-start.5 = (bf16[256,256]{1,0:T(8,128)(2,1)S(1)}, bf16[256,256]{1,0:T(8,128)(2,1)}, u32[]{:S(2)}) copy-start(bf16[256,256]{1,0:T(8,128)(2,1)} %param.20) | copy-start | bytes 393220
  7.2 74.2 %all-gather.9.cloned.1.call-start = ((), (), s32[]{:S(2)}) async-start(), calls=%async_computation.1 | async-start | bytes 1114112 | tf_op jit(solution)/shard_map/all_gather | solution.py:162
  9.1 147.0 %all-gather.19.cloned.1.call-start = ((), (), s32[]{:S(2)}) async-start(), calls=%async_computation.6 | async-start | bytes 1114112 | tf_op jit(solution)/shard_map/all_gather | solution.py:165
  10.9 220.6 %all-gather.11.cloned.1.call-start = ((), (), s32[]{:S(2)}) async-start(), calls=%async_computation.2 | async-start | bytes 1114112 | tf_op jit(solution)/shard_map/all_gather | solution.py:163
  12.7 294.0 %all-gather.17.cloned.1.call-start = ((), (), s32[]{:S(2)}) async-start(), calls=%async_computation.5 | async-start | bytes 1114112 | tf_op jit(solution)/shard_map/all_gather | solution.py:164
  14.5 373.5 %all-gather.13.cloned.1.call-start = ((), (), s32[]{:S(2)}) async-start(), calls=%async_computation.3 | async-start | bytes 2228224 | tf_op jit(solution)/shard_map/all_gather | solution.py:166
  15.5 16.1 %copy-start.6 = (bf16[256,256]{1,0:T(8,128)(2,1)S(1)}, bf16[256,256]{1,0:T(8,128)(2,1)}, u32[]{:S(2)}) copy-start(bf16[256,256]{1,0:T(8,128)(2,1)} %param.18) | copy-start | bytes 393220
  17.4 15.4 %copy-start.18 = (s32[128]{0:T(128)S(1)}, s32[128]{0:T(128)}, u32[]{:S(2)}) copy-start(s32[128]{0:T(128)} %param.16) | copy-start | bytes 1540
  17.4 47.1 %copy-start.8 = (bf16[128,256]{1,0:T(8,128)(2,1)S(1)}, bf16[128,256]{1,0:T(8,128)(2,1)}, u32[]{:S(2)}) copy-start(bf16[128,256]{1,0:T(8,128)(2,1)} %param.13) | copy-start | bytes 196612
  17.4 450.4 %all-gather.15.cloned.1.call-start = ((), (), s32[]{:S(2)}) async-start(), calls=%async_computation.4 | async-start | bytes 2228224 | tf_op jit(solution)/shard_map/all_gather | solution.py:167
  17.8 47.7 %copy-start.10 = (bf16[128,256]{1,0:T(8,128)(2,1)S(1)}, bf16[128,256]{1,0:T(8,128)(2,1)}, u32[]{:S(2)}) copy-start(bf16[128,256]{1,0:T(8,128)(2,1)} %param.14) | copy-start | bytes 196612
  19.4 46.9 %all-to-all-start = ((bf16[128,16,128]{2,0,1:T(8,128)(2,1)}), bf16[128,16,128]{2,0,1:T(8,128)(2,1)}, u32[]{:S(2)}, u32[]{:S(2)}) async-start(bf16[128,16,128]{2,0,1:T(8,128)(2,1)} %copy_bitcast_fusion), calls=%async_computation | async-start | bytes 1048576 | tf_op jit(solution)/shard_map/all_to_all | solution.py:41
  31.4 703.7 %all-gather.21.cloned.1.call-start = ((), (), s32[]{:S(2)}) async-start(), calls=%async_computation.7 | async-start | bytes 2162688 | tf_op jit(solution)/shard_map/all_gather | solution.py:9
  468.4 5.2 copy-start.16
  482.1 6.7 copy-start.4
  486.5 3.5 copy-start.1
  492.0 5.2 copy-start.16
  505.7 7.5 %copy-start.4 = (f32[128,4,64]{0,2,1:T(8,128)S(1)}, f32[128,4,64]{0,2,1:T(8,128)}, u32[]{:S(2)}) copy-start(f32[128,4,64]{0,2,1:T(8,128)} %get-tuple-element.916) | copy-start | bytes 393220 | tf_op jit(solution)/shard_map/while
  510.9 3.5 copy-start.1
  513.2 2.3 copy-start.2
  516.4 5.2 copy-start.16
  530.1 7.5 %copy-start.4 = (f32[128,4,64]{0,2,1:T(8,128)S(1)}, f32[128,4,64]{0,2,1:T(8,128)}, u32[]{:S(2)}) copy-start(f32[128,4,64]{0,2,1:T(8,128)} %get-tuple-element.916) | copy-start | bytes 393220 | tf_op jit(solution)/shard_map/while
  535.2 3.5 copy-start.1
  537.5 2.3 copy-start.2
  540.8 5.2 copy-start.16
  554.5 7.5 %copy-start.4 = (f32[128,4,64]{0,2,1:T(8,128)S(1)}, f32[128,4,64]{0,2,1:T(8,128)}, u32[]{:S(2)}) copy-start(f32[128,4,64]{0,2,1:T(8,128)} %get-tuple-element.916) | copy-start | bytes 393220 | tf_op jit(solution)/shard_map/while
  559.6 3.5 copy-start.1
  561.9 2.3 copy-start.2
  565.1 5.2 copy-start.16
  578.8 7.5 %copy-start.4 = (f32[128,4,64]{0,2,1:T(8,128)S(1)}, f32[128,4,64]{0,2,1:T(8,128)}, u32[]{:S(2)}) copy-start(f32[128,4,64]{0,2,1:T(8,128)} %get-tuple-element.916) | copy-start | bytes 393220 | tf_op jit(solution)/shard_map/while
  584.0 3.5 copy-start.1
  586.3 2.3 copy-start.2
  589.5 5.2 copy-start.16
  603.2 7.5 %copy-start.4 = (f32[128,4,64]{0,2,1:T(8,128)S(1)}, f32[128,4,64]{0,2,1:T(8,128)}, u32[]{:S(2)}) copy-start(f32[128,4,64]{0,2,1:T(8,128)} %get-tuple-element.916) | copy-start | bytes 393220 | tf_op jit(solution)/shard_map/while
  608.3 3.5 copy-start.1
  610.7 2.3 copy-start.2
  613.9 5.2 copy-start.16
  627.6 7.5 %copy-start.4 = (f32[128,4,64]{0,2,1:T(8,128)S(1)}, f32[128,4,64]{0,2,1:T(8,128)}, u32[]{:S(2)}) copy-start(f32[128,4,64]{0,2,1:T(8,128)} %get-tuple-element.916) | copy-start | bytes 393220 | tf_op jit(solution)/shard_map/while
  632.7 3.5 copy-start.1
  635.0 2.3 copy-start.2
  638.3 5.2 copy-start.16
  651.9 7.5 %copy-start.4 = (f32[128,4,64]{0,2,1:T(8,128)S(1)}, f32[128,4,64]{0,2,1:T(8,128)}, u32[]{:S(2)}) copy-start(f32[128,4,64]{0,2,1:T(8,128)} %get-tuple-element.916) | copy-start | bytes 393220 | tf_op jit(solution)/shard_map/while
  657.1 3.5 copy-start.1
  659.4 2.3 copy-start.2
  662.6 5.9 copy-start.7
  662.6 5.9 copy-start.9
  664.5 72.5 %copy-start.11 = (bf16[128,256]{1,0:T(8,128)(2,1)S(1)}, bf16[128,256]{1,0:T(8,128)(2,1)}, u32[]{:S(2)}) copy-start(bf16[128,256]{1,0:T(8,128)(2,1)} %param.14) | copy-start | bytes 196612
  (49 other events, 56.8 us)
Sparse Core Ops, SparseCore 0:
  10.7 70.6 all-gather.8
  83.5 72.5 all-gather.18
  158.2 73.2 all-gather.10
  233.4 73.2 all-gather.16
  308.6 79.3 all-gather.12
  389.9 77.8 all-gather.14
  666.6 68.5 all-gather.20
